TPU v7x, 128 devices: a whole 4x4x4 slice. The times are simulated.
128 devices in a mesh: row: 8 (over y, z_hi), col: 16 (over x, z_lo, core).
Axes of the slice: x: 4, y: 4, z: 4 (z_hi: 2, z_lo: 2; z = z_hi * 2 + z_lo), core: 2. Of those that a mesh axis runs over, the one named last changes fastest.
Arguments:
- adjacency: bfloat16 [32768, 32768], P('row', 'col'), as said below
- tile_mask: int32 [256, 256], P('row', 'col'), may hold values from 0 to 1, as said below
- out_grad: bfloat16 [32768, 256], P(('row', 'col')), may hold values from -6 to 6
- pre_two: bfloat16 [32768, 256], P(('row', 'col')), may hold values from -6 to 6
- hidden: bfloat16 [32768, 256], P(('col', 'row')), may hold values from -24 to 24
- pre_one: bfloat16 [32768, 256], P(('col', 'row')), may hold values from -6 to 6
- features: bfloat16 [32768, 256], P(('row', 'col')), may hold values from -6 to 6
- w_two: bfloat16 [256, 256], replicated, may hold values from -0.375 to 0.375
- w_one: bfloat16 [256, 256], replicated, may hold values from -0.375 to 0.375
Outputs:
- node_grad: bfloat16 [32768, 256], P(('row', 'col'))
- weight_grad_one: float32 [256, 256], replicated
- weight_grad_two: float32 [256, 256], replicated
Inputs may be any that keep to these rules, and one draw needn't show every extreme that they name: adjacency is symmetric and nonnegative. tile_mask is symmetric and every diagonal tile is 1.
All inputs are finite; a program needn't handle non-finite values.
Results may differ from a plain program's by a relative error of at most 0.02.
Values may be sent and summed in bfloat16 or wider, within the bound.
A program may use at most 128 MiB of HBM per device.

v0:
```python
import jax
import jax.numpy as jnp
from jax import lax
from jax.sharding import PartitionSpec as P


def tile_pick(count, tile_size, tile_total):
    node_ids = lax.broadcasted_iota(jnp.int32, (count, 1), 0)
    tile_ids = lax.broadcasted_iota(jnp.int32, (1, tile_total), 1)
    return (node_ids // tile_size == tile_ids).astype(jnp.bfloat16)


def local(adjacency, tile_mask, out_grad, pre_two, hidden, pre_one, features, w_two, w_one):
    tile_rows, tile_cols = tile_mask.shape
    tile_size = adjacency.shape[0] // tile_rows
    mask_values = tile_mask.astype(jnp.bfloat16)
    shard_nodes = out_grad.shape[0]
    weight_scale = 4.0 * shard_nodes ** (-0.5)
    contract_rows = (((0,), (0,)), ((), ()))
    contract_cols = (((1,), (1,)), ((), ()))
    grad_two = jnp.where(pre_two > 0, out_grad, jnp.zeros_like(out_grad))
    shard_rows = lax.all_gather(grad_two, "col", axis=0, tiled=True)
    count = shard_rows.shape[0]
    strip_rows = adjacency
    picker = tile_pick(count, tile_size, tile_rows)
    strip_mask = jnp.dot(picker, mask_values, preferred_element_type=jnp.float32).astype(
        jnp.bfloat16
    )
    strip_rows = (strip_rows.reshape(count, tile_cols, tile_size) * strip_mask[:, :, None]).reshape(
        count, adjacency.shape[1]
    )
    column_part = lax.dot_general(
        strip_rows, shard_rows, contract_rows, preferred_element_type=jnp.float32
    )
    column_part = column_part.astype(jnp.bfloat16).astype(jnp.float32)
    prop_two = lax.psum_scatter(
        column_part.astype(jnp.bfloat16), "row", scatter_dimension=0, tiled=True
    )
    back_grad = lax.dot_general(prop_two, w_two, contract_cols, preferred_element_type=jnp.float32)
    grad_one = jnp.where(pre_one > 0, back_grad, jnp.zeros_like(back_grad)).astype(jnp.bfloat16)
    shard_rows = lax.all_gather(grad_one, "row", axis=0, tiled=True)
    count = shard_rows.shape[0]
    strip_cols = adjacency
    picker = tile_pick(count, tile_size, tile_cols)
    strip_mask = lax.dot_general(
        mask_values, picker, contract_cols, preferred_element_type=jnp.float32
    ).astype(jnp.bfloat16)
    strip_cols = (strip_cols.reshape(tile_rows, tile_size, count) * strip_mask[:, None, :]).reshape(
        adjacency.shape[0], count
    )
    row_part = jnp.dot(strip_cols, shard_rows, preferred_element_type=jnp.float32)
    term_two = lax.dot_general(hidden, prop_two, contract_rows, preferred_element_type=jnp.float32)
    summed_two = lax.psum(term_two, ("row", "col"))
    row_part = row_part.astype(jnp.bfloat16).astype(jnp.float32)
    prop_one = lax.psum_scatter(
        row_part.astype(jnp.bfloat16), "col", scatter_dimension=0, tiled=True
    )
    term_one = lax.dot_general(
        features, prop_one, contract_rows, preferred_element_type=jnp.float32
    )
    node_grad = lax.dot_general(
        prop_one, w_one, contract_cols, preferred_element_type=jnp.float32
    ).astype(jnp.bfloat16)
    summed_one = lax.psum(term_one, ("row", "col"))
    return (node_grad, summed_one * weight_scale, summed_two * weight_scale)


def solution(mesh):
    return jax.shard_map(
        local,
        mesh=mesh,
        in_specs=(
            P("row", "col"),
            P("row", "col"),
            P(("row", "col"), None),
            P(("row", "col"), None),
            P(("col", "row"), None),
            P(("col", "row"), None),
            P(("row", "col"), None),
            P(),
            P(),
        ),
        out_specs=(P(("row", "col"), None), P(), P()),
        check_vma=False,
    )
```

profile of v0, /device:TPU:1, one launch (start us, length us, event | category | flops | bytes accessed | tf_op | source)
XLA Modules:
  0.0 437.8 jit_solution(10373811274106707431)
XLA Ops:
  7.2 0.0 copy-start
  7.2 0.0 all-gather.3.cloned.1.call-start
  7.2 1.7 compare_select_fusion
  8.9 0.0 all-gather.3.cloned.1.call-update
  8.9 0.0 reduce-scatter.3.cloned.1.call-start
  9.0 0.9 convolution_convert_fusion.1
  9.9 0.5 copy.15
  10.4 37.4 %all-gather.3.cloned.1.call-done = bf16[4096,256]{1,0:T(8,128)(2,1)} async-done(((bf16[256,256]{1,0:T(8,128)(2,1)}), bf16[4096,256]{1,0:T(8,128)(2,1)}) %all-gather.3.cloned.1.call-update) | async-done | bytes 2097168 | tf_op jit(solution)/shard_map/all_gather | solution.py:22
  47.7 18.8 %mul.31 = bf16[4096,16,128]{2,1,0:T(8,128)(2,1)} broadcast(bf16[4096,16]{1,0:T(8,128)(2,1)S(1)} %copy.15), dimensions={0,1} | broadcast | bytes 16908288 | tf_op jit(solution)/shard_map/mul | solution.py:29
  66.5 0.0 copy-done.7
  66.5 14.3 %fusion.2 = bf16[2048,256]{1,0:T(8,128)(2,1)} fusion(bf16[4096,256]{1,0:T(8,128)(2,1)S(1)} %copy-done.7, bf16[4096,2048]{1,0:T(8,128)(2,1)} %param.9, bf16[512,8,16,128]{3,2,1,0:T(8,128)(2,1)} %bitcast.25), kind=kOutput, calls=%fused_computation.6 | convolution fusion | flops 4303880192 | bytes 36700160 | tf_op jit(solution)/shard_map/dot_general | solution.py:32
  80.9 0.0 reduce-scatter.3.cloned.1.call-update
  80.9 0.0 all-gather.5.cloned.1.call-start
  80.9 70.7 %reduce-scatter.3.cloned.1.call-done = bf16[256,256]{1,0:T(8,128)(2,1)} async-done(((bf16[2048,256]{1,0:T(8,128)(2,1)}), bf16[256,256]{1,0:T(8,128)(2,1)}) %reduce-scatter.3.cloned.1.call-update) | async-done | bytes 131088 | tf_op jit(solution)/shard_map/reduce_scatter | solution.py:36
  151.6 1.8 fusion.4
  153.4 0.0 all-gather.5.cloned.1.call-update
  153.4 0.0 reduce-scatter.5.cloned.1.call-start
  153.5 0.5 fusion.3
  154.0 13.9 %bitcast_multiply_fusion.2 = bf16[4096,2048]{1,0:T(8,128)(2,1)} fusion(bf16[4096,2048]{1,0:T(8,128)(2,1)} %param.9, bf16[32,2048]{1,0:T(8,128)(2,1)S(1)} %fusion.3), kind=kLoop, calls=%fused_computation.3 | loop fusion | flops 8388608 | bytes 33685504 | tf_op jit(solution)/shard_map/mul | solution.py:48
  167.9 33.0 %all-gather.5.cloned.1.call-done = bf16[2048,256]{1,0:T(8,128)(2,1)} async-done(((bf16[256,256]{1,0:T(8,128)(2,1)}), bf16[2048,256]{1,0:T(8,128)(2,1)}) %all-gather.5.cloned.1.call-update) | async-done | bytes 1048592 | tf_op jit(solution)/shard_map/all_gather | solution.py:41
  201.0 11.9 %convolution_convert_fusion = bf16[4096,256]{1,0:T(8,128)(2,1)} fusion(bf16[4096,2048]{1,0:T(8,128)(2,1)} %bitcast_multiply_fusion.2, bf16[2048,256]{1,0:T(8,128)(2,1)} %all-gather.5.cloned.1.call-done), kind=kOutput, calls=%fused_computation.4 | convolution fusion | flops 4296015872 | bytes 19922944 | tf_op jit(solution)/shard_map/dot_general | solution.py:51
  212.9 0.0 reduce-scatter.5.cloned.1.call-update
  212.9 0.0 all-reduce.3.cloned.1.call-start
  213.0 0.9 convolution_bitcast_fusion
  213.9 60.4 %reduce-scatter.5.cloned.1.call-done = bf16[256,256]{1,0:T(8,128)(2,1)} async-done(((bf16[4096,256]{1,0:T(8,128)(2,1)}), bf16[256,256]{1,0:T(8,128)(2,1)}) %reduce-scatter.5.cloned.1.call-update) | async-done | bytes 131088 | tf_op jit(solution)/shard_map/reduce_scatter | solution.py:55
  274.3 1.8 convolution_bitcast_fusion.1
  276.2 0.0 all-reduce.3.cloned.1.call-update
  276.2 1.8 convolution_convert_fusion.3
  278.0 150.5 %all-reduce.3.cloned.1.call-done = (f32[256,256]{0,1:T(8,128)}, f32[256,256]{0,1:T(8,128)}) async-done(((f32[256,256]{0,1:T(8,128)}, f32[256,256]{0,1:T(8,128)}), (f32[256,256]{0,1:T(8,128)}, f32[256,256]{0,1:T(8,128)})) %all-reduce.3.cloned.1.call-update) | async-done | bytes 524304 | tf_op jit(solution)/shard_map/psum | solution.py:64
  428.5 1.1 broadcast_multiply_fusion
  429.6 0.8 copy.16
  430.4 0.8 copy.17
  (16 shorter events, 0.0 us)
Async XLA Ops:
  7.2 144.5 %copy-start = (bf16[256,256]{1,0:T(8,128)(2,1)S(1)}, bf16[256,256]{1,0:T(8,128)(2,1)}, u32[]{:S(2)}) copy-start(bf16[256,256]{1,0:T(8,128)(2,1)} %param.16) | copy-start | bytes 393220
  7.2 40.5 %all-gather.3.cloned.1.call-start = ((), (), s32[]{:S(2)}) async-start(), calls=%async_computation.2 | async-start | bytes 2228224 | tf_op jit(solution)/shard_map/all_gather | solution.py:22
  8.9 142.7 %reduce-scatter.3.cloned.1.call-start = ((), (), s32[]{:S(2)}) async-start(), calls=%async_computation.3 | async-start | bytes 1179648 | tf_op jit(solution)/shard_map/reduce_scatter | solution.py:36
  47.7 18.8 %copy-start.7 = (bf16[4096,256]{1,0:T(8,128)(2,1)S(1)}, bf16[4096,256]{1,0:T(8,128)(2,1)}, u32[]{:S(2)}) copy-start(bf16[4096,256]{1,0:T(8,128)(2,1)} %all-gather.3.cloned.1.call-done) | copy-start | bytes 6291460
  66.5 85.1 %copy-start.3 = (bf16[256,256]{1,0:T(8,128)(2,1)S(1)}, bf16[256,256]{1,0:T(8,128)(2,1)}, u32[]{:S(2)}) copy-start(bf16[256,256]{1,0:T(8,128)(2,1)} %param.14) | copy-start | bytes 393220
  66.5 87.0 %copy-start.6 = (s32[32,16]{0,1:T(8,128)S(1)}, s32[32,16]{0,1:T(8,128)}, u32[]{:S(2)}) copy-start(s32[32,16]{0,1:T(8,128)} %param.10) | copy-start | bytes 6148
  80.9 120.1 %all-gather.5.cloned.1.call-start = ((), (), s32[]{:S(2)}) async-start(), calls=%async_computation.4 | async-start | bytes 1179648 | tf_op jit(solution)/shard_map/all_gather | solution.py:41
  153.4 120.9 %reduce-scatter.5.cloned.1.call-start = ((), (), s32[]{:S(2)}) async-start(), calls=%async_computation.5 | async-start | bytes 2228224 | tf_op jit(solution)/shard_map/reduce_scatter | solution.py:55
  167.9 45.0 %copy-start.1 = (bf16[256,256]{1,0:T(8,128)(2,1)S(1)}, bf16[256,256]{1,0:T(8,128)(2,1)}, u32[]{:S(2)}) copy-start(bf16[256,256]{1,0:T(8,128)(2,1)} %reduce-scatter.3.cloned.1.call-done) | copy-start | bytes 393220
  167.9 45.0 %copy-start.4 = (bf16[256,256]{1,0:T(8,128)(2,1)S(1)}, bf16[256,256]{1,0:T(8,128)(2,1)}, u32[]{:S(2)}) copy-start(bf16[256,256]{1,0:T(8,128)(2,1)} %param.13) | copy-start | bytes 393220
  167.9 106.4 %copy-start.5 = (bf16[256,256]{1,0:T(8,128)(2,1)S(1)}, bf16[256,256]{1,0:T(8,128)(2,1)}, u32[]{:S(2)}) copy-start(bf16[256,256]{1,0:T(8,128)(2,1)} %param.15) | copy-start | bytes 393220
  167.9 108.2 %copy-start.2 = (bf16[256,256]{1,0:T(8,128)(2,1)S(1)}, bf16[256,256]{1,0:T(8,128)(2,1)}, u32[]{:S(2)}) copy-start(bf16[256,256]{1,0:T(8,128)(2,1)} %param.17) | copy-start | bytes 393220
  212.9 215.6 %all-reduce.3.cloned.1.call-start = ((), (), s32[]{:S(2)}) async-start(), calls=%async_computation.6 | async-start | bytes 1048576 | tf_op jit(solution)/shard_map/psum | solution.py:64
Sparse Core Ops, SparseCore 0:
  10.3 37.4 all-gather.2
  81.0 70.5 reduce-scatter.2
  154.5 46.3 all-gather.4
  213.0 61.2 reduce-scatter.4
  279.7 148.7 all-reduce.2
where the time goes:
time: 438 us
  waiting for transfers between devices  352 us (80%)
  matrix products  33.9 us (8%)
  local copies, waits for them, and re-layouts  21 us (5%)
  other arithmetic  16.7 us (4%)
  between operations  13.9 us (3%)
    psum x1, waiting for transfers between devices, local(): summed_one = lax.psum(term_one, ('row', 'col'))  151 us
    reduce_scatter x1, waiting for transfers between devices, local(): lax.psum_scatter(column_part.astype(jnp.bfloat16), 'row', scatter_dimensi...  70.7 us
    reduce_scatter x1, waiting for transfers between devices, local(): lax.psum_scatter(row_part.astype(jnp.bfloat16), 'col', scatter_dimension=...  60.4 us
    all_gather x1, waiting for transfers between devices, local(): shard_rows = lax.all_gather(grad_two, 'col', axis=0, tiled=True)  37.4 us
    all_gather x1, waiting for transfers between devices, local(): shard_rows = lax.all_gather(grad_one, 'row', axis=0, tiled=True)  33 us
    mul x1, local copies, waits for them, and re-layouts, local(): strip_rows.reshape(count, tile_cols, tile_size) * strip_mask[:, :, None]  18.8 us
    dot_general x1, matrix products, local(): lax.dot_general(strip_rows, shard_rows, contract_rows, preferred_element_...  14.3 us
    mul x1, other arithmetic, local(): strip_cols.reshape(tile_rows, tile_size, count) * strip_mask[:, None, :]  13.9 us
  transfers between devices with their start and end apart: 5, of which 5 were waited for; matrix products, arithmetic and copies ran while one was open for 4% of the time, Pallas kernels for 0%

commit v1 on v0

v1 whole, which is shorter than its diff:
```python
import functools

import jax
import jax.numpy as jnp
from jax import lax
from jax.experimental import pallas as pl
from jax.experimental.pallas import tpu as pltpu
from jax.sharding import PartitionSpec as P

MESH = pl.DeviceIdType.MESH
F32 = jnp.float32
BF16 = jnp.bfloat16
NT = (((1,), (1,)), ((), ()))
TN = (((0,), (0,)), ((), ()))


def mm(a, b):
    return jnp.dot(a, b, preferred_element_type=F32)


def kernel(
    n_row, n_col, tile, scale,
    adj_hbm, mask_hbm, og_hbm, p2_hbm, hid_hbm, p1_hbm, feat_hbm, w2_hbm, w1_hbm,
    node_out, wg1_out, wg2_out,
    graph, mask_v, mexp, small, gt, acc, sb, rb, gc, acc2, sd, rs, rd, e_src, e_r1, e_r2, e_sum, e_out,
    load_sem, gload_sem, a_s, a_r, b_s, b_r, c_s, c_r, ds_s, ds_r, d_s, d_r,
    e1_s, e1_r, e2_s, e2_r, e3_s, e3_r,
):
    row, col = lax.axis_index("row"), lax.axis_index("col")
    s = og_hbm.shape[0]
    h = s // 2
    y, zh = row // 2, lax.rem(row, 2)
    x, zl, core = col // 4, lax.rem(col // 2, 2), lax.rem(col, 2)

    def xor(a, k, bits):
        out = a * 0
        for i in range(bits):
            bit = lax.rem(a // (1 << i), 2)
            out = out + ((1 - bit) if (k >> i) & 1 else bit) * (1 << i)
        return out

    def col_at(dx, dz=0, dc=0):
        zz = (1 - zl) if dz else zl
        cc = (1 - core) if dc else core
        return lax.rem(x + dx + 4, 4) * 4 + zz * 2 + cc

    def row_at(dy, dz=0):
        zz = (1 - zh) if dz else zh
        return lax.rem(y + dy + 4, 4) * 2 + zz

    order = [
        (0, 0, 0), (0, 0, 1), (0, 1, 0), (-1, 0, 0), (1, 0, 0), (0, 1, 1), (-1, 0, 1), (1, 0, 1),
        (-1, 1, 0), (1, 1, 0), (-1, 1, 1), (1, 1, 1), (2, 0, 0), (2, 0, 1), (2, 1, 0), (2, 1, 1),
    ]

    names = [(og_hbm, 0), (p2_hbm, 1), (w2_hbm, 2), (p1_hbm, 3), (hid_hbm, 4), (feat_hbm, 5), (w1_hbm, 6)]
    loads = [pltpu.make_async_copy(ref, small.at[i], load_sem.at[i]) for ref, i in names]
    mload = pltpu.make_async_copy(mask_hbm, mask_v, load_sem.at[7])
    loads[0].start()
    loads[1].start()
    mload.start()
    gloads = []
    for i, o in enumerate(order):
        at = pl.ds(pl.multiple_of(col_at(*o) * s, s), s)
        cp = pltpu.make_async_copy(adj_hbm.at[at, :], graph.at[at, :], gload_sem.at[i])
        cp.start()
        gloads.append(cp)
    for cp in loads[2:]:
        cp.start()

    barrier = pltpu.get_barrier_semaphore()
    for k in range(1, n_col):
        pl.semaphore_signal(barrier, inc=1, device_id=(row, xor(col, k, 4)), device_id_type=MESH)
    for k in range(1, n_row):
        pl.semaphore_signal(barrier, inc=1, device_id=(xor(row, k, 3), col), device_id_type=MESH)

    loads[0].wait()
    loads[1].wait()
    own = jnp.where(small[1].astype(F32) > 0, small[0].astype(F32), 0.0)
    gt[col] = own.T.astype(BF16)
    mload.wait()
    width = mexp.shape[1]
    pick = (
        lax.broadcasted_iota(jnp.int32, (mask_v.shape[1], width), 1) // tile
        == lax.broadcasted_iota(jnp.int32, (mask_v.shape[1], width), 0)
    ).astype(F32)
    mexp[...] = mm(mask_v[...].astype(F32).astype(BF16), pick.astype(BF16))
    pl.semaphore_wait(barrier, n_col + n_row - 2)

    pending = []

    def send(src, dst, ss, rr, k, dev):
        cp = pltpu.make_async_remote_copy(
            src_ref=src, dst_ref=dst, send_sem=ss.at[k], recv_sem=rr.at[k],
            device_id=dev, device_id_type=MESH,
        )
        cp.start()
        pending.append(cp)
        return cp

    lo, hi = pl.ds(0, h), pl.ds(h, h)
    a_cp = {}

    def a_send(k, o, to, part=None):
        ref = gt.at[col_at(*o)] if part is None else gt.at[col_at(*o), part]
        a_cp[k] = send(ref, ref, a_s, a_r, k, (row, col_at(*to)))

    zp, xp, xm, sib = (0, 1, 0), (1, 0, 0), (-1, 0, 0), (0, 0, 1)
    a_send(0, (0, 0, 0), zp)
    a_send(1, (0, 0, 0), xp)
    a_send(2, (0, 0, 0), xm)
    a_send(3, (0, 0, 0), sib)

    def mask_chunk(i):
        o = order[i]
        gloads[i].wait()
        j = col_at(*o)
        for t in range(s // tile):
            m = mexp[pl.ds(j * (s // tile) + t, 1), :]
            m16 = jnp.broadcast_to(m, (16, width)).astype(BF16)

            @pl.loop(0, tile // 16)
            def _(g):
                at = pl.ds(pl.multiple_of(j * s + t * tile + g * 16, 16), 16)
                graph[at, :] = graph[at, :] * m16

    def mm1(idx, first=False):
        for i in idx:
            mask_chunk(i)
        js = [col_at(*order[i]) for i in idx]

        @pl.loop(0, n_row)
        def _(d):
            at = pl.ds(pl.multiple_of(d * s, s), s)
            total = None
            for j in js:
                p = mm(gt[j], graph[pl.ds(pl.multiple_of(j * s, s), s), at])
                total = p if total is None else total + p
            acc[d] = total if first else acc[d] + total

    mm1([0], True)
    a_cp[3].wait_recv()
    mm1([1])
    a_cp[0].wait_recv()
    a_send(4, (0, 1, 0), xp)
    a_send(5, (0, 1, 0), xm)
    a_send(6, (0, 1, 0), sib)
    a_cp[1].wait_recv()
    a_send(7, (-1, 0, 0), xp, lo)
    a_send(8, (-1, 0, 0), sib)
    a_cp[2].wait_recv()
    a_send(9, (1, 0, 0), xm, hi)
    a_send(10, (1, 0, 0), sib)
    mm1([2, 3])
    a_cp[6].wait_recv()
    mm1([4, 5])
    a_cp[4].wait_recv()
    a_send(11, (-1, 1, 0), xp, lo)
    a_send(12, (-1, 1, 0), sib)
    a_cp[5].wait_recv()
    a_send(13, (1, 1, 0), xm, hi)
    a_send(14, (1, 1, 0), sib)
    a_cp[8].wait_recv()
    a_cp[10].wait_recv()
    mm1([6, 7])
    mm1([8, 9])
    a_cp[7].wait_recv()
    a_cp[9].wait_recv()
    a_send(15, (2, 0, 0), sib)
    a_cp[12].wait_recv()
    a_cp[14].wait_recv()
    mm1([10, 11])
    a_cp[11].wait_recv()
    a_cp[13].wait_recv()
    a_send(16, (2, 1, 0), sib)
    a_cp[15].wait_recv()
    mm1([12, 13])
    a_cp[16].wait_recv()
    mm1([14, 15])

    def scatter(part, sbuf, rbuf, ss, rr, ring, slot):
        cp = {}

        def go(k, o, half, value, to):
            ref = sbuf.at[slot(*o), lo if half == 0 else hi]
            ref[...] = value.astype(BF16)
            cp[k] = send(ref, rbuf.at[k], ss, rr, k, ring(*to))

        for k, dz in ((0, 1), (2, 0)):
            go(k, (2, dz), 0, part(2, dz, 0), (1, 0))
            go(k + 1, (2, dz), 1, part(2, dz, 1), (-1, 0))
        for k, dz in ((4, 1), (6, 0)):
            go(k, (1, dz), 1, part(1, dz, 1), (1, 0))
            go(k + 1, (-1, dz), 0, part(-1, dz, 0), (-1, 0))
        for k, dz, b in ((8, 1, 0), (10, 0, 2)):
            cp[b].wait_recv()
            go(k, (1, dz), 0, part(1, dz, 0) + rbuf[b].astype(F32), (1, 0))
            cp[b + 1].wait_recv()
            go(k + 1, (-1, dz), 1, part(-1, dz, 1) + rbuf[b + 1].astype(F32), (-1, 0))
        for k in (4, 5, 8, 9):
            cp[k].wait_recv()
        go(12, (0, 1), 0, part(0, 1, 0) + rbuf[5].astype(F32) + rbuf[8].astype(F32), (0, 1))
        go(13, (0, 1), 1, part(0, 1, 1) + rbuf[4].astype(F32) + rbuf[9].astype(F32), (0, 1))
        for k in (6, 7, 10, 11):
            cp[k].wait_recv()
        top = part(0, 0, 0) + rbuf[7].astype(F32) + rbuf[10].astype(F32)
        low = part(0, 0, 1) + rbuf[6].astype(F32) + rbuf[11].astype(F32)
        cp[12].wait_recv()
        top = top + rbuf[12].astype(F32)
        cp[13].wait_recv()
        low = low + rbuf[13].astype(F32)
        return jnp.concatenate([top, low], axis=0)

    def part_b(dy, dz, half):
        return acc[row_at(dy, dz), lo if half == 0 else hi]

    prop_t = scatter(part_b, sb, rb, b_s, b_r, lambda dy, dz: (row_at(dy, dz), col), row_at)
    prop_two = prop_t.T.astype(BF16)

    for cp in loads[2:]:
        cp.wait()
    back = lax.dot_general(prop_two, small[2], NT, preferred_element_type=F32)
    gc[row] = jnp.where(small[3].astype(F32) > 0, back, 0.0).astype(BF16)
    c_cp = {}

    def c_send(k, o, to, part=None):
        ref = gc.at[row_at(*o)] if part is None else gc.at[row_at(*o), part]
        c_cp[k] = send(ref, ref, c_s, c_r, k, (row_at(*to), col))

    c_send(0, (0, 0), (0, 1))
    c_send(1, (0, 0), (1, 0))
    c_send(2, (0, 0), (-1, 0))

    e1, e2, e3 = {}, {}, {}

    def reduce_start(w, term):
        e_src[w] = term.reshape(e_src.shape[1:])
        for k in range(1, n_col):
            peer = xor(col, k, 4)
            e1[w, k] = send(e_src.at[w, peer], e_r1.at[w, k], e1_s.at[w], e1_r.at[w], k, (row, peer))

    def reduce_middle(w):
        total = e_src[w, col]
        for k in range(1, n_col):
            e1[w, k].wait_recv()
            total = total + e_r1[w, k]
        e_sum[w] = total
        for k in range(1, n_row):
            e2[w, k] = send(e_sum.at[w], e_r2.at[w, k], e2_s.at[w], e2_r.at[w], k, (xor(row, k, 3), col))

    def reduce_last(w):
        total = e_sum[w]
        for k in range(1, n_row):
            e2[w, k].wait_recv()
            total = total + e_r2[w, k]
        e_out[w, col] = total * scale
        for k in range(1, n_col):
            peer = xor(col, k, 4)
            e3[w, k] = send(e_out.at[w, col], e_out.at[w, col], e3_s.at[w], e3_r.at[w], k, (row, peer))

    def reduce_end(w, out):
        for k in range(1, n_col):
            e3[w, k].wait_recv()
        out[...] = e_out[w].reshape(out.shape)

    reduce_start(0, lax.dot_general(small[4], prop_two, TN, preferred_element_type=F32))

    def mm2(os, first=False):
        rs_ = [row_at(*o) for o in os]

        @pl.loop(0, n_col)
        def _(j):
            at = pl.ds(pl.multiple_of(j * s, s), s)
            total = None
            for r in rs_:
                p = mm(graph[at, pl.ds(pl.multiple_of(r * s, s), s)], gc[r])
                total = p if total is None else total + p
            acc2[j] = total if first else acc2[j] + total

    mm2([(0, 0)], True)
    c_cp[0].wait_recv()
    c_send(3, (0, 1), (1, 0))
    c_send(4, (0, 1), (-1, 0))
    c_cp[1].wait_recv()
    c_send(5, (-1, 0), (1, 0), lo)
    c_cp[2].wait_recv()
    c_send(6, (1, 0), (-1, 0), hi)
    mm2([(0, 1), (-1, 0)])
    c_cp[3].wait_recv()
    c_send(7, (-1, 1), (1, 0), lo)
    c_cp[4].wait_recv()
    c_send(8, (1, 1), (-1, 0), hi)
    mm2([(1, 0), (-1, 1)])
    reduce_middle(0)
    c_cp[5].wait_recv()
    c_cp[6].wait_recv()
    mm2([(1, 1), (2, 0)])
    c_cp[7].wait_recv()
    c_cp[8].wait_recv()

    last = row_at(2, 1)
    last_cols = pl.ds(pl.multiple_of(last * s, s), s)
    ring_order = [(2, 1), (2, 0), (1, 1), (-1, 1), (1, 0), (-1, 0), (0, 1), (0, 0)]
    ds_cp = {}
    for i, (dx, dz) in enumerate(ring_order):
        j = col_at(dx, dz, 1)
        total = acc2[j] + mm(graph[pl.ds(pl.multiple_of(j * s, s), s), last_cols], gc[last])
        sd[j] = total.astype(BF16)
        ds_cp[dx, dz] = send(sd.at[j], rs.at[i], ds_s, ds_r, i, (row, col_at(0, 0, 1)))
    for dx, dz in ring_order:
        j = col_at(dx, dz, 0)
        acc2[j] = acc2[j] + mm(graph[pl.ds(pl.multiple_of(j * s, s), s), last_cols], gc[last])

    arrived = set()

    def part_d(dx, dz, half):
        if (dx, dz) not in arrived:
            ds_cp[dx, dz].wait_recv()
            arrived.add((dx, dz))
        at = lo if half == 0 else hi
        return acc2[col_at(dx, dz), at] + rs[ring_order.index((dx, dz)), at].astype(F32)

    reduce_last(0)
    prop_one = scatter(part_d, sd, rd, d_s, d_r, lambda dx, dz: (row, col_at(dx, dz)), col_at).astype(BF16)
    reduce_start(1, lax.dot_general(small[5], prop_one, TN, preferred_element_type=F32))
    node_out[...] = lax.dot_general(prop_one, small[6], NT, preferred_element_type=F32).astype(BF16)
    reduce_end(0, wg2_out)
    reduce_middle(1)
    reduce_last(1)
    reduce_end(1, wg1_out)
    for cp in pending:
        cp.wait_send()


def local(adjacency, tile_mask, out_grad, pre_two, hidden, pre_one, features, w_two, w_one):
    n_row, n_col = lax.axis_size("row"), lax.axis_size("col")
    rows, cols = adjacency.shape
    s, f = out_grad.shape
    tile = rows // tile_mask.shape[0]
    scale = 4.0 * s ** (-0.5)
    h = s // 2
    sl = f // n_col
    dma = pltpu.SemaphoreType.DMA
    return pl.pallas_call(
        functools.partial(kernel, n_row, n_col, tile, scale),
        out_shape=(
            jax.ShapeDtypeStruct((s, f), BF16),
            jax.ShapeDtypeStruct((f, f), F32),
            jax.ShapeDtypeStruct((f, f), F32),
        ),
        in_specs=[pl.BlockSpec(memory_space=pl.ANY)] * 9,
        out_specs=[pl.BlockSpec(memory_space=pltpu.VMEM)] * 3,
        scratch_shapes=[
            pltpu.VMEM((rows, cols), BF16),
            pltpu.VMEM(tile_mask.shape, jnp.int32),
            pltpu.VMEM((tile_mask.shape[0], cols), F32),
            pltpu.VMEM((7, s, f), BF16),
            pltpu.VMEM((n_col, f, s), BF16),
            pltpu.VMEM((n_row, f, s), F32),
            pltpu.VMEM((n_row, f, s), BF16),
            pltpu.VMEM((14, h, f), BF16),
            pltpu.VMEM((n_row, s, f), BF16),
            pltpu.VMEM((n_col, s, f), F32),
            pltpu.VMEM((n_col, s, f), BF16),
            pltpu.VMEM((n_row, s, f), BF16),
            pltpu.VMEM((14, h, f), BF16),
            pltpu.VMEM((2, n_col, sl, f), F32),
            pltpu.VMEM((2, n_col, sl, f), F32),
            pltpu.VMEM((2, n_row, sl, f), F32),
            pltpu.VMEM((2, sl, f), F32),
            pltpu.VMEM((2, n_col, sl, f), F32),
            dma((8,)), dma((n_col,)), dma((17,)), dma((17,)), dma((14,)), dma((14,)), dma((9,)), dma((9,)),
            dma((8,)), dma((8,)), dma((14,)), dma((14,)),
            dma((2, n_col)), dma((2, n_col)), dma((2, n_row)), dma((2, n_row)), dma((2, n_col)), dma((2, n_col)),
        ],
        compiler_params=pltpu.CompilerParams(
            collective_id=0, has_side_effects=True, vmem_limit_bytes=56 << 20
        ),
    )(adjacency, tile_mask, out_grad, pre_two, hidden, pre_one, features, w_two, w_one)


def solution(mesh):
    return jax.shard_map(
        local,
        mesh=mesh,
        in_specs=(
            P("row", "col"),
            P("row", "col"),
            P(("row", "col"), None),
            P(("row", "col"), None),
            P(("col", "row"), None),
            P(("col", "row"), None),
            P(("row", "col"), None),
            P(),
            P(),
        ),
        out_specs=(P(("row", "col"), None), P(), P()),
        check_vma=False,
    )
```

time: 438 us -> 109 us (0.25)
  waiting for transfers between devices: 352 us -> 0 us
  Pallas kernels: 0 us -> 102 us
  matrix products: 33.9 us -> 0 us
  other arithmetic: 16.7 us -> 0 us
  local copies, waits for them, and re-layouts: 21 us -> 6.28 us
  between operations: 13.9 us -> 0.64 us
    psum x1 -> x0, waiting for transfers between devices: 151 us -> none  [local(): summed_one = lax.psum(term_one, ('row', 'col'))]
    reduce_scatter x2 -> x0, waiting for transfers between devices: 131 us -> none  [the longest x1 70.7 us: local(): lax.psum_scatter(column_part.astype(jnp.bfloat16), 'row', scatter_dimensi...]
    pallas_call x0 -> x1, Pallas kernels: none -> 102 us  [local(): pl.pallas_call(functools.partial(kernel, n_row, n_col, tile, scale), out_...]
    all_gather x2 -> x0, waiting for transfers between devices: 70.4 us -> none  [the longest x1 37.4 us: local(): shard_rows = lax.all_gather(grad_two, 'col', axis=0, tiled=True)]
    dot_general x8 -> x0, matrix products: 33.9 us -> none  [the longest x1 14.3 us: local(): lax.dot_general(strip_rows, shard_rows, contract_rows, preferred_element_...]
    mul x1 -> x0, local copies, waits for them, and re-layouts: 18.8 us -> none  [local(): strip_rows.reshape(count, tile_cols, tile_size) * strip_mask[:, :, None]]
    mul x2 -> x0, other arithmetic: 15 us -> none  [the longest x1 13.9 us: local(): strip_cols.reshape(tile_rows, tile_size, count) * strip_mask[:, None, :]]
    unnamed x18 -> x4, local copies, waits for them, and re-layouts: 1.71 us -> 6.28 us
  transfers between devices with their start and end apart: 5 -> 0, of which waited for: 5 -> 0; matrix products, arithmetic and copies ran while one was open for 4% -> 0% of each run, Pallas kernels for 0% -> 0%
where the time goes in v1:
time: 109 us
  Pallas kernels  102 us (94%)
  local copies, waits for them, and re-layouts  6.28 us (6%)
    pallas_call x1, Pallas kernels, local(): pl.pallas_call(functools.partial(kernel, n_row, n_col, tile, scale), out_...  102 us
    unnamed x4, local copies, waits for them, and re-layouts  6.28 us

profile of v1, /device:TPU:1, one launch (start us, length us, event | category | flops | bytes accessed | tf_op | source)
XLA Modules:
  0.0 109.2 jit_solution(5078580828821880729)
XLA Ops:
  0.6 1.4 %copy.12.mask_hbm = s32[32,16]{1,0:T(8,128)} copy(s32[32,16]{0,1:T(8,128)} %param.10) | data formatting | bytes 4096 | tf_op args[1]
  2.0 102.3 %shard_map.112 = (bf16[256,256]{1,0:T(8,128)(2,1)}, f32[256,256]{1,0:T(8,128)}, f32[256,256]{1,0:T(8,128)}) custom-call(bf16[4096,2048]{1,0:T(8,128)(2,1)} %adj_hbm.1, s32[32,16]{1,0:T(8,128)} %copy.12.mask_hbm, bf16[256,256]{1,0:T(8,128)(2,1)} %og_hbm.1, bf16[256,256]{1,0:T(8,128)(2,1)} %p2_hbm.1, bf16[256,256]{1,0:T(8,128)(2,1)} %hid_hbm.1, ...), custom_call_target="tpu_custom_call" | custom-call | tf_op jit(solution)/shard_map/pallas_call | solution.py:344
  104.3 1.6 %copy.16 = bf16[256,256]{1,0:T(8,128)(2,1)} copy(bf16[256,256]{1,0:T(8,128)(2,1)} %get-tuple-element.6) | data formatting | bytes 262144
  105.8 1.7 %copy.17 = f32[256,256]{1,0:T(8,128)} copy(f32[256,256]{1,0:T(8,128)} %get-tuple-element.7) | data formatting | bytes 524288
  107.5 1.7 %copy.18 = f32[256,256]{1,0:T(8,128)} copy(f32[256,256]{1,0:T(8,128)} %get-tuple-element.8) | data formatting | bytes 524288

commit v2 on v1

v2 whole, which is shorter than its diff:
```python
import functools

import jax
import jax.numpy as jnp
from jax import lax
from jax.experimental import pallas as pl
from jax.experimental.pallas import tpu as pltpu
from jax.sharding import PartitionSpec as P

MESH = pl.DeviceIdType.MESH
F32 = jnp.float32
BF16 = jnp.bfloat16
NT = (((1,), (1,)), ((), ()))
TN = (((0,), (0,)), ((), ()))


def mm(a, b):
    return jnp.dot(a, b, preferred_element_type=F32)


def kernel(
    n_row, n_col, tile, scale,
    adj_hbm, mask_hbm, og_hbm, p2_hbm, hid_hbm, p1_hbm, feat_hbm, w2_hbm, w1_hbm,
    node_out, wg1_out, wg2_out,
    graph, mask_v, mexp, small, gt, ft, acc, sb, rb, gc, acc2, sd, rs, rd,
    e_src, e_sib, e_half, e_r1, e_r2, e_sum, e_out,
    load_sem, gload_sem, s_s, s_r, f_s, f_r, a_s, a_r, b_s, b_r, c_s, c_r, ds_s, ds_r, d_s, d_r,
    e0_s, e0_r, e1_s, e1_r, e2_s, e2_r, e3_s, e3_r,
):
    row, col = lax.axis_index("row"), lax.axis_index("col")
    s = og_hbm.shape[0]
    h = s // 2
    y, zh = row // 2, lax.rem(row, 2)
    x, zl, core = col // 4, lax.rem(col // 2, 2), lax.rem(col, 2)

    def xor(a, k, bits):
        out = a * 0
        for i in range(bits):
            bit = lax.rem(a // (1 << i), 2)
            out = out + ((1 - bit) if (k >> i) & 1 else bit) * (1 << i)
        return out

    def col_at(dx, dz=0, dc=0):
        zz = (1 - zl) if dz else zl
        cc = (1 - core) if dc else core
        return lax.rem(x + dx + 4, 4) * 4 + zz * 2 + cc

    def row_at(dy, dz=0):
        zz = (1 - zh) if dz else zh
        return lax.rem(y + dy + 4, 4) * 2 + zz

    order = [
        (0, 0, 0), (0, 0, 1), (-1, 0, 0), (1, 0, 0), (-1, 0, 1), (1, 0, 1), (0, 1, 0), (0, 1, 1),
        (2, 0, 0), (2, 0, 1), (-1, 1, 0), (1, 1, 0), (-1, 1, 1), (1, 1, 1), (2, 1, 0), (2, 1, 1),
    ]

    names = [(og_hbm, 0), (p2_hbm, 1), (w2_hbm, 2), (p1_hbm, 3), (hid_hbm, 4), (feat_hbm, 5), (w1_hbm, 6)]
    loads = [pltpu.make_async_copy(ref, small.at[i], load_sem.at[i]) for ref, i in names]
    mload = pltpu.make_async_copy(mask_hbm, mask_v, load_sem.at[7])
    barrier = pltpu.get_barrier_semaphore()
    steps = ((1, 0), (-1, 0), (2, 0), (0, 1))
    hello = [(row, col_at(0, 0, 1))] + [(row, col_at(*o)) for o in steps] + [(row_at(*o), col) for o in steps]
    for dev in hello:
        pl.semaphore_signal(barrier, inc=1, device_id=dev, device_id_type=MESH)
    loads[0].start()
    loads[1].start()
    mload.start()
    gloads = []
    for i, o in enumerate(order):
        at = pl.ds(pl.multiple_of(col_at(*o) * s, s), s)
        cp = pltpu.make_async_copy(adj_hbm.at[at, :], graph.at[at, :], gload_sem.at[i])
        cp.start()
        gloads.append(cp)
    for cp in loads[2:]:
        cp.start()

    loads[0].wait()
    loads[1].wait()
    own = jnp.where(small[1].astype(F32) > 0, small[0].astype(F32), 0.0)
    gt[col] = own.T.astype(BF16)
    mload.wait()
    width = mexp.shape[1]
    pick = (
        lax.broadcasted_iota(jnp.int32, (mask_v.shape[0], width), 1) // tile
        == lax.broadcasted_iota(jnp.int32, (mask_v.shape[0], width), 0)
    ).astype(F32)
    mexp[...] = mm(mask_v[...].astype(F32).T.astype(BF16), pick.astype(BF16))
    pl.semaphore_wait(barrier, len(hello))

    pending = []

    def send(src, dst, ss, rr, k, dev):
        cp = pltpu.make_async_remote_copy(
            src_ref=src, dst_ref=dst, send_sem=ss.at[k], recv_sem=rr.at[k],
            device_id=dev, device_id_type=MESH,
        )
        cp.start()
        pending.append(cp)
        return cp

    lo, hi = pl.ds(0, h), pl.ds(h, h)
    halves = (lo, hi)

    def gather(buf, slot, dev, ss, rr):
        cp = {}

        def go(k, o, half, to):
            ref = buf.at[slot(*o), halves[half]]
            cp[k] = send(ref, ref, ss, rr, k, dev(*to))

        def start():
            go(0, (0, 0), 0, (0, 1))
            for k, d in ((1, 1), (2, -1), (3, 2)):
                go(k, (0, 0), 1, (d, 0))
            for k, d in ((4, 1), (5, -1), (6, 2)):
                go(k, (0, 0), 0, (d, 0))
            go(7, (0, 0), 1, (0, 1))

        def forward():
            cp[0].wait_recv()
            for k, d in ((8, 1), (9, -1), (10, 2)):
                go(k, (0, 1), 0, (d, 0))
            for k, d in ((1, -1), (2, 1), (3, 2)):
                cp[k].wait_recv()
                go(k + 10, (d, 0), 1, (0, 1))

        def near(d):
            cp[{-1: 4, 1: 5, 2: 6}[d]].wait_recv()

        def pair():
            cp[7].wait_recv()

        def far(d):
            k = {-1: 8, 1: 9, 2: 10}[d]
            cp[k].wait_recv()
            cp[k + 3].wait_recv()

        return start, forward, near, pair, far

    def scatter(part, sbuf, rbuf, slot, dev, ss, rr):
        cp = {}

        def go(k, o, half, value, to):
            ref = sbuf.at[slot(*o), halves[half]]
            ref[...] = value.astype(BF16)
            cp[k] = send(ref, rbuf.at[k], ss, rr, k, dev(*to))

        def got(k):
            cp[k].wait_recv()
            return rbuf[k].astype(F32)

        def one():
            for k, d in ((0, 1), (1, -1), (2, 2), (3, 0)):
                go(k, (d, 1), 1, part(d, 1, 1), (0, 1))
                if d:
                    go(k + 4, (d, 1), 0, part(d, 1, 0), (d, 0))
            for k, d in ((7, 1), (8, -1), (9, 2)):
                go(k, (d, 0), 0, part(d, 0, 0), (d, 0))

        def two():
            for k, d in ((0, 1), (1, -1), (2, 2)):
                go(k + 10, (d, 0), 1, part(d, 0, 1) + got(k), (d, 0))

        def three():
            go(13, (0, 1), 0, part(0, 1, 0) + got(4) + got(5) + got(6), (0, 1))

        def four():
            low = part(0, 0, 1) + got(3)
            top = part(0, 0, 0) + got(7) + got(8) + got(9)
            low = low + got(10) + got(11) + got(12)
            top = top + got(13)
            return jnp.concatenate([top, low], axis=0)

        return one, two, three, four

    def weight_reduce(w, inner, outer, me, both):
        cp = {}
        sib_dev = (row, col_at(0, 0, 1))

        def zero(term):
            e_src[w] = term.reshape(e_src.shape[1:])
            cp["a"] = send(e_src.at[w, 1 - core], e_sib.at[w], e0_s, e0_r, w, sib_dev)

        def one():
            cp["a"].wait_recv()
            e_half[w] = e_src[w, core] + e_sib[w]
            for k in range(1, n_row):
                cp[1, k] = send(e_half.at[w, xor(me, k, 3)], e_r1.at[w, k], e1_s.at[w], e1_r.at[w], k, inner(k))

        def two():
            total = e_half[w, me]
            for k in range(1, n_row):
                cp[1, k].wait_recv()
                total = total + e_r1[w, k]
            e_sum[w] = total
            for k in range(1, n_row):
                cp[2, k] = send(e_sum.at[w], e_r2.at[w, k], e2_s.at[w], e2_r.at[w], k, outer(k))

        def three():
            total = e_sum[w]
            for k in range(1, n_row):
                cp[2, k].wait_recv()
                total = total + e_r2[w, k]
            e_out[w, core, me] = total * scale
            ref = e_out.at[w, core, me]
            for k in range(1, n_row):
                cp[3, k] = send(ref, ref, e3_s.at[w, 0], e3_r.at[w, 0], k, inner(k))
            if both:
                cp["b"] = send(ref, ref, e0_s, e0_r, 2 + w, sib_dev)
                for k in range(1, n_row):
                    cp[4, k] = send(ref, ref, e3_s.at[w, 1], e3_r.at[w, 1], k, (inner(k)[0], col_at(0, 0, 1)))

        def four():
            for k in range(1, n_row):
                cp[3, k].wait_recv()
                if both:
                    cp[4, k].wait_recv()
            if both:
                return
            ref = e_out.at[w, core]
            cp["b"] = send(ref, ref, e0_s, e0_r, 2 + w, sib_dev)

        def five(out):
            cp["b"].wait_recv()
            out[...] = e_out[w].reshape(out.shape)

        return zero, one, two, three, four, five

    def row_dev(k):
        return (xor(row, k, 3), col)

    def col_dev(k):
        return (row, xor(col // 2, k, 3) * 2 + core)

    def in_row(dy, dz):
        return (row_at(dy, dz), col)

    def in_col(dx, dz):
        return (row, col_at(dx, dz))

    sib_dev = (row, col_at(0, 0, 1))
    s_cp = {}

    def to_sibling(buf, o, k):
        ref = buf.at[col_at(*o)]
        s_cp[k] = send(ref, ref, s_s, s_r, k, sib_dev)

    start, forward, near, pair, far = gather(gt, col_at, in_col, a_s, a_r)
    start()
    to_sibling(gt, (0, 0), 0)

    def mask_chunk(i):
        o = order[i]
        gloads[i].wait()
        j = col_at(*o)
        for t in range(s // tile):
            m = mexp[pl.ds(j * (s // tile) + t, 1), :]
            m16 = jnp.broadcast_to(m, (16, width)).astype(BF16)

            @pl.loop(0, tile // 16)
            def _(g):
                at = pl.ds(pl.multiple_of(j * s + t * tile + g * 16, 16), 16)
                graph[at, :] = graph[at, :] * m16

    def mm1(idx, first=False):
        js = [col_at(*order[i]) for i in idx]

        @pl.loop(0, n_row, unroll=8)
        def _(d):
            at = pl.ds(pl.multiple_of(d * s, s), s)
            total = None
            for j in js:
                p = mm(gt[j], graph[pl.ds(pl.multiple_of(j * s, s), s), at])
                total = p if total is None else total + p
            acc[d] = total if first else acc[d] + total

    mask_chunk(0)
    mask_chunk(1)
    s_cp[0].wait_recv()
    mm1([0, 1], True)
    forward()
    for i in (2, 3, 4, 5):
        mask_chunk(i)
    near(-1)
    to_sibling(gt, (-1, 0), 1)
    near(1)
    to_sibling(gt, (1, 0), 2)
    mm1([2, 3])
    pair()
    to_sibling(gt, (0, 1), 3)
    for i in (6, 7, 8, 9):
        mask_chunk(i)
    s_cp[1].wait_recv()
    s_cp[2].wait_recv()
    mm1([4, 5])
    near(2)
    to_sibling(gt, (2, 0), 4)
    s_cp[3].wait_recv()
    mm1([6, 7])
    for i in (10, 11, 12, 13, 14, 15):
        mask_chunk(i)
    far(-1)
    to_sibling(gt, (-1, 1), 5)
    far(1)
    to_sibling(gt, (1, 1), 6)
    s_cp[4].wait_recv()
    mm1([8, 9])
    far(2)
    to_sibling(gt, (2, 1), 7)
    s_cp[5].wait_recv()
    mm1([10, 11])
    s_cp[6].wait_recv()
    mm1([12, 13])
    s_cp[7].wait_recv()

    summed = set()

    def part_b(dy, dz, half):
        if (dy, dz) not in summed:
            summed.add((dy, dz))
            d = row_at(dy, dz)
            at = pl.ds(pl.multiple_of(d * s, s), s)
            j, jj = col_at(*order[14]), col_at(*order[15])
            acc[d] = (
                acc[d]
                + mm(gt[j], graph[pl.ds(pl.multiple_of(j * s, s), s), at])
                + mm(gt[jj], graph[pl.ds(pl.multiple_of(jj * s, s), s), at])
            )
        return acc[row_at(dy, dz), halves[half]]

    one, two, three, four = scatter(part_b, sb, rb, row_at, in_row, b_s, b_r)
    one()
    for cp in loads[2:]:
        cp.wait()
    ft[col] = small[5].astype(F32).T.astype(BF16)
    f_cp = {}

    def f_send(k, o, to):
        ref = ft.at[col_at(*o)]
        f_cp[k] = send(ref, ref, f_s, f_r, k, in_col(*to))

    f_send(0, (0, 0), (0, 1))
    f_send(1, (0, 0), (1, 0))
    f_send(2, (0, 0), (-1, 0))
    f_send(3, (0, 0), (2, 0))
    to_sibling(ft, (0, 0), 8)
    two()
    three()
    prop_two = four().T.astype(BF16)

    back = lax.dot_general(prop_two, small[2], NT, preferred_element_type=F32)
    gc[row] = jnp.where(small[3].astype(F32) > 0, back, 0.0).astype(BF16)
    start, forward, near, pair, far = gather(gc, row_at, in_row, c_s, c_r)
    start()
    w2_0, w2_1, w2_2, w2_3, w2_4, w2_5 = weight_reduce(0, col_dev, row_dev, col // 2, False)
    w2_0(lax.dot_general(small[4], prop_two, TN, preferred_element_type=F32))

    def mm2(os, first=False):
        rs_ = [row_at(*o) for o in os]

        @pl.loop(0, n_col, unroll=8)
        def _(j):
            at = pl.ds(pl.multiple_of(j * s, s), s)
            total = None
            for r in rs_:
                p = mm(graph[at, pl.ds(pl.multiple_of(r * s, s), s)], gc[r])
                total = p if total is None else total + p
            acc2[j] = total if first else acc2[j] + total

    f_cp[0].wait_recv()
    for k, d in ((4, 1), (5, -1), (6, 2)):
        f_send(k, (0, 1), (d, 0))
    to_sibling(ft, (0, 1), 9)
    w2_1()
    forward()
    mm2([(0, 0)], True)
    for k, d in ((1, -1), (2, 1), (3, 2)):
        f_cp[k].wait_recv()
        to_sibling(ft, (d, 0), 9 + k)
    near(-1)
    near(1)
    mm2([(-1, 0), (1, 0)])
    w2_2()
    near(2)
    pair()
    mm2([(2, 0), (0, 1)])
    for k, d in ((4, -1), (5, 1), (6, 2)):
        f_cp[k].wait_recv()
        to_sibling(ft, (d, 1), 9 + k)
    far(-1)
    far(1)
    mm2([(-1, 1), (1, 1)])
    w2_3()
    far(2)

    last = row_at(2, 1)
    last_cols = pl.ds(pl.multiple_of(last * s, s), s)
    ring_order = [(1, 1), (-1, 1), (2, 1), (0, 1), (1, 0), (-1, 0), (2, 0), (0, 0)]
    ds_cp = {}
    for i, (dx, dz) in enumerate(ring_order):
        j = col_at(dx, dz, 1)
        total = acc2[j] + mm(graph[pl.ds(pl.multiple_of(j * s, s), s), last_cols], gc[last])
        sd[j] = total.astype(BF16)
        ds_cp[dx, dz] = send(sd.at[j], rs.at[i], ds_s, ds_r, i, sib_dev)
    for dx, dz in ring_order:
        j = col_at(dx, dz, 0)
        acc2[j] = acc2[j] + mm(graph[pl.ds(pl.multiple_of(j * s, s), s), last_cols], gc[last])

    arrived = set()

    def part_d(dx, dz, half):
        if (dx, dz) not in arrived:
            ds_cp[dx, dz].wait_recv()
            arrived.add((dx, dz))
        at = halves[half]
        return acc2[col_at(dx, dz), at] + rs[ring_order.index((dx, dz)), at].astype(F32)

    one, two, three, four = scatter(part_d, sd, rd, col_at, in_col, d_s, d_r)
    one()
    for k in range(8, 16):
        s_cp[k].wait_recv()
    term = None
    for dx, dz in ring_order:
        j, jj = col_at(dx, dz, 0), col_at(dx, dz, 1)
        p = mm(ft[j], acc2[j].astype(BF16)) + mm(ft[jj], sd[jj])
        term = p if term is None else term + p
    w1_0, w1_1, w1_2, w1_3, w1_4, w1_5 = weight_reduce(1, row_dev, col_dev, row, True)
    w1_0(term)
    w2_4()
    w1_1()
    two()
    w1_2()
    three()
    w1_3()
    prop_one = four().astype(BF16)
    node_out[...] = lax.dot_general(prop_one, small[6], NT, preferred_element_type=F32).astype(BF16)
    w2_5(wg2_out)
    w1_4()
    w1_5(wg1_out)
    for cp in pending:
        cp.wait_send()


def finish(node_in, wg1_in, wg2_in, node_out, wg1_out, wg2_out, node, wg, sem):
    refs = ((node_in, node, node_out), (wg1_in, wg.at[0], wg1_out), (wg2_in, wg.at[1], wg2_out))
    ins = [pltpu.make_async_copy(a, b, sem.at[0, i]) for i, (a, b, _) in enumerate(refs)]
    outs = [pltpu.make_async_copy(b, c, sem.at[1, i]) for i, (_, b, c) in enumerate(refs)]
    for cp in ins:
        cp.start()
    for cp, out in zip(ins, outs):
        cp.wait()
        out.start()
    for out in outs:
        out.wait()


def local(adjacency, tile_mask, out_grad, pre_two, hidden, pre_one, features, w_two, w_one):
    n_row, n_col = lax.axis_size("row"), lax.axis_size("col")
    rows, cols = adjacency.shape
    s, f = out_grad.shape
    tile = rows // tile_mask.shape[0]
    scale = 4.0 * s ** (-0.5)
    h = s // 2
    sl = f // n_col
    dma = pltpu.SemaphoreType.DMA
    outs = pl.pallas_call(
        functools.partial(kernel, n_row, n_col, tile, scale),
        out_shape=(
            jax.ShapeDtypeStruct((s, f), BF16),
            jax.ShapeDtypeStruct((f, f), F32),
            jax.ShapeDtypeStruct((f, f), F32),
        ),
        in_specs=[pl.BlockSpec(memory_space=pl.ANY)] * 9,
        out_specs=[pl.BlockSpec(memory_space=pltpu.VMEM)] * 3,
        scratch_shapes=[
            pltpu.VMEM((rows, cols), BF16),
            pltpu.VMEM(tile_mask.shape[::-1], jnp.int32),
            pltpu.VMEM((tile_mask.shape[0], cols), F32),
            pltpu.VMEM((7, s, f), BF16),
            pltpu.VMEM((n_col, f, s), BF16),
            pltpu.VMEM((n_col, f, s), BF16),
            pltpu.VMEM((n_row, f, s), F32),
            pltpu.VMEM((n_row, f, s), BF16),
            pltpu.VMEM((14, h, f), BF16),
            pltpu.VMEM((n_row, s, f), BF16),
            pltpu.VMEM((n_col, s, f), F32),
            pltpu.VMEM((n_col, s, f), BF16),
            pltpu.VMEM((n_row, s, f), BF16),
            pltpu.VMEM((14, h, f), BF16),
            pltpu.VMEM((2, 2, n_row, sl, f), F32),
            pltpu.VMEM((2, n_row, sl, f), F32),
            pltpu.VMEM((2, n_row, sl, f), F32),
            pltpu.VMEM((2, n_row, sl, f), F32),
            pltpu.VMEM((2, n_row, sl, f), F32),
            pltpu.VMEM((2, sl, f), F32),
            pltpu.VMEM((2, 2, n_row, sl, f), F32),
            dma((8,)), dma((n_col,)), dma((16,)), dma((16,)), dma((7,)), dma((7,)),
            dma((14,)), dma((14,)), dma((14,)), dma((14,)), dma((14,)), dma((14,)),
            dma((8,)), dma((8,)), dma((14,)), dma((14,)),
            dma((4,)), dma((4,)), dma((2, n_row)), dma((2, n_row)), dma((2, n_row)), dma((2, n_row)),
            dma((2, 2, n_row)), dma((2, 2, n_row)),
        ],
        compiler_params=pltpu.CompilerParams(
            collective_id=0, has_side_effects=True, vmem_limit_bytes=56 << 20
        ),
    )(adjacency, tile_mask.T, out_grad, pre_two, hidden, pre_one, features, w_two, w_one)
    return pl.pallas_call(
        finish,
        out_shape=tuple(jax.ShapeDtypeStruct(o.shape, o.dtype) for o in outs),
        in_specs=[pl.BlockSpec(memory_space=pl.ANY)] * 3,
        out_specs=[pl.BlockSpec(memory_space=pl.ANY)] * 3,
        scratch_shapes=[
            pltpu.VMEM(outs[0].shape, BF16), pltpu.VMEM((2,) + outs[1].shape, F32), dma((2, 3)),
        ],
        compiler_params=pltpu.CompilerParams(vmem_limit_bytes=56 << 20),
    )(*outs)


def solution(mesh):
    return jax.shard_map(
        local,
        mesh=mesh,
        in_specs=(
            P("row", "col"),
            P("row", "col"),
            P(("row", "col"), None),
            P(("row", "col"), None),
            P(("col", "row"), None),
            P(("col", "row"), None),
            P(("row", "col"), None),
            P(),
            P(),
        ),
        out_specs=(P(("row", "col"), None), P(), P()),
        check_vma=False,
    )
```

time: 109 us -> 80.3 us (0.74)
  Pallas kernels: 102 us -> 79.5 us
  local copies, waits for them, and re-layouts: 6.28 us -> 0 us
    pallas_call x1, Pallas kernels: 102 us -> 77.7 us  [local(): pl.pallas_call(functools.partial(kernel, n_row, n_col, tile, scale), out_...]
    unnamed x4 -> x0, local copies, waits for them, and re-layouts: 6.28 us -> none
    pallas_call x0 -> x1, Pallas kernels: none -> 1.86 us  [local(): pl.pallas_call(finish, out_shape=tuple((jax.ShapeDtypeStruct(o.shape, o.d...]
where the time goes in v2:
time: 80.3 us; the launch traced here: 80.2 us
  Pallas kernels  79.5 us (99%)
    pallas_call x1, Pallas kernels, local(): pl.pallas_call(functools.partial(kernel, n_row, n_col, tile, scale), out_...  77.7 us
    pallas_call x1, Pallas kernels, local(): pl.pallas_call(finish, out_shape=tuple((jax.ShapeDtypeStruct(o.shape, o.d...  1.86 us

profile of v2, /device:TPU:1, one launch (start us, length us, event | category | flops | bytes accessed | tf_op | source)
XLA Modules:
  0.0 80.2 jit_solution(5555785234194620062)
XLA Ops:
  0.6 77.7 %shard_map.112 = (bf16[256,256]{1,0:T(8,128)(2,1)}, f32[256,256]{1,0:T(8,128)}, f32[256,256]{1,0:T(8,128)}) custom-call(bf16[4096,2048]{1,0:T(8,128)(2,1)} %adj_hbm.1, s32[16,32]{1,0:T(8,128)} %bitcast.1, bf16[256,256]{1,0:T(8,128)(2,1)} %og_hbm.1, bf16[256,256]{1,0:T(8,128)(2,1)} %p2_hbm.1, bf16[256,256]{1,0:T(8,128)(2,1)} %hid_hbm.1, ...), custom_call_target="tpu_custom_call" | custom-call | tf_op jit(solution)/shard_map/pallas_call | solution.py:466
  78.3 1.9 %shard_map.113 = (bf16[256,256]{1,0:T(8,128)(2,1)}, f32[256,256]{1,0:T(8,128)}, f32[256,256]{1,0:T(8,128)}) custom-call(bf16[256,256]{1,0:T(8,128)(2,1)} %get-tuple-element.6.node_in, f32[256,256]{1,0:T(8,128)} %get-tuple-element.7.wg1_in, f32[256,256]{1,0:T(8,128)} %get-tuple-element.8.wg2_in), custom_call_target="tpu_custom_call" | custom-call | tf_op jit(solution)/shard_map/pallas_call | solution.py:507

commit v3 on v2

--- a/solution.py
+++ b/solution.py
@@ -23,22 +23,15 @@
     adj_hbm, mask_hbm, og_hbm, p2_hbm, hid_hbm, p1_hbm, feat_hbm, w2_hbm, w1_hbm,
     node_out, wg1_out, wg2_out,
     graph, mask_v, mexp, small, gt, ft, acc, sb, rb, gc, acc2, sd, rs, rd,
-    e_src, e_sib, e_half, e_r1, e_r2, e_sum, e_out,
+    e_src, e_sib, e_half, e_r, e_all, e_out,
     load_sem, gload_sem, s_s, s_r, f_s, f_r, a_s, a_r, b_s, b_r, c_s, c_r, ds_s, ds_r, d_s, d_r,
-    e0_s, e0_r, e1_s, e1_r, e2_s, e2_r, e3_s, e3_r,
+    e0_s, e0_r, e1_s, e1_r,
 ):
     row, col = lax.axis_index("row"), lax.axis_index("col")
     s = og_hbm.shape[0]
     h = s // 2
     y, zh = row // 2, lax.rem(row, 2)
     x, zl, core = col // 4, lax.rem(col // 2, 2), lax.rem(col, 2)
-
-    def xor(a, k, bits):
-        out = a * 0
-        for i in range(bits):
-            bit = lax.rem(a // (1 << i), 2)
-            out = out + ((1 - bit) if (k >> i) & 1 else bit) * (1 << i)
-        return out
 
     def col_at(dx, dz=0, dc=0):
         zz = (1 - zl) if dz else zl
@@ -173,64 +166,77 @@
 
         return one, two, three, four
 
-    def weight_reduce(w, inner, outer, me, both):
+    ring = ((0, 1), (1, -1), (2, 2))
+    flips = ((0, 0, 1), (1, 1, 0), (2, 1, 1))
+
+    def weight_reduce(w, p, q, inner, outer, both):
         cp = {}
         sib_dev = (row, col_at(0, 0, 1))
 
-        def zero(term):
-            e_src[w] = term.reshape(e_src.shape[1:])
+        def zero_send(term):
+            e_src[w, 1 - core] = term.reshape(e_src.shape[2:])
             cp["a"] = send(e_src.at[w, 1 - core], e_sib.at[w], e0_s, e0_r, w, sib_dev)
+
+        def zero_keep(term):
+            e_src[w, core] = term.reshape(e_src.shape[2:])
 
         def one():
             cp["a"].wait_recv()
-            e_half[w] = e_src[w, core] + e_sib[w]
-            for k in range(1, n_row):
-                cp[1, k] = send(e_half.at[w, xor(me, k, 3)], e_r1.at[w, k], e1_s.at[w], e1_r.at[w], k, inner(k))
+            total = e_src[w, core] + e_sib[w]
+            e_src[w, core] = total
+            e_half[w] = total.astype(BF16)
+            for k, d in ring:
+                src = e_half.at[w, lax.rem(p + d + 4, 4)]
+                cp[1, k] = send(src, e_r.at[w, k], e1_s.at[w, 0], e1_r.at[w, 0], k, inner(d))
+
+        def share(stage, at, total, peers):
+            ref = e_all.at[w, stage, at]
+            ref[...] = total.astype(BF16)
+            for k, dev in peers:
+                cp[stage + 2, k] = send(ref, ref, e1_s.at[w, stage + 1], e1_r.at[w, stage + 1], k, dev)
+
+        def gathered(stage):
+            for k in range(3):
+                cp[stage + 2, k].wait_recv()
+            v = [e_all[w, stage, k].astype(F32) for k in range(4)]
+            return (v[0] + v[1]) + (v[2] + v[3])
 
         def two():
-            total = e_half[w, me]
-            for k in range(1, n_row):
+            total = e_src[w, core, p]
+            for k in range(3):
                 cp[1, k].wait_recv()
-                total = total + e_r1[w, k]
-            e_sum[w] = total
-            for k in range(1, n_row):
-                cp[2, k] = send(e_sum.at[w], e_r2.at[w, k], e2_s.at[w], e2_r.at[w], k, outer(k))
+                total = total + e_r[w, k].astype(F32)
+            share(0, zh * 2 + zl, total, [(k, (row_at(0, dh), col_at(0, dl))) for k, dh, dl in flips])
 
         def three():
-            total = e_sum[w]
-            for k in range(1, n_row):
-                cp[2, k].wait_recv()
-                total = total + e_r2[w, k]
-            e_out[w, core, me] = total * scale
-            ref = e_out.at[w, core, me]
-            for k in range(1, n_row):
-                cp[3, k] = send(ref, ref, e3_s.at[w, 0], e3_r.at[w, 0], k, inner(k))
+            share(1, q, gathered(0), [(k, outer(d)) for k, d in ring])
+
+        def four():
+            e_out[w, core, p] = (gathered(1) * scale).astype(BF16)
+            ref = e_out.at[w, core, p]
+            for k, d in ring:
+                cp[4, k] = send(ref, ref, e1_s.at[w, 3], e1_r.at[w, 3], k, inner(d))
             if both:
                 cp["b"] = send(ref, ref, e0_s, e0_r, 2 + w, sib_dev)
-                for k in range(1, n_row):
-                    cp[4, k] = send(ref, ref, e3_s.at[w, 1], e3_r.at[w, 1], k, (inner(k)[0], col_at(0, 0, 1)))
-
-        def four():
-            for k in range(1, n_row):
-                cp[3, k].wait_recv()
+                for k, d in ring:
+                    dev = (inner(d)[0], col_at(0, 0, 1))
+                    cp[5, k] = send(ref, ref, e1_s.at[w, 4], e1_r.at[w, 4], k, dev)
+
+        def five():
+            for k in range(3):
+                cp[4, k].wait_recv()
                 if both:
-                    cp[4, k].wait_recv()
+                    cp[5, k].wait_recv()
             if both:
                 return
             ref = e_out.at[w, core]
             cp["b"] = send(ref, ref, e0_s, e0_r, 2 + w, sib_dev)
 
-        def five(out):
+        def six(out):
             cp["b"].wait_recv()
-            out[...] = e_out[w].reshape(out.shape)
-
-        return zero, one, two, three, four, five
-
-    def row_dev(k):
-        return (xor(row, k, 3), col)
-
-    def col_dev(k):
-        return (row, xor(col // 2, k, 3) * 2 + core)
+            out[...] = e_out[w].reshape(out.shape).astype(F32)
+
+        return zero_send, zero_keep, one, two, three, four, five, six
 
     def in_row(dy, dz):
         return (row_at(dy, dz), col)
@@ -339,12 +345,12 @@
         ref = ft.at[col_at(*o)]
         f_cp[k] = send(ref, ref, f_s, f_r, k, in_col(*to))
 
+    two()
     f_send(0, (0, 0), (0, 1))
     f_send(1, (0, 0), (1, 0))
     f_send(2, (0, 0), (-1, 0))
     f_send(3, (0, 0), (2, 0))
     to_sibling(ft, (0, 0), 8)
-    two()
     three()
     prop_two = four().T.astype(BF16)
 
@@ -352,8 +358,11 @@
     gc[row] = jnp.where(small[3].astype(F32) > 0, back, 0.0).astype(BF16)
     start, forward, near, pair, far = gather(gc, row_at, in_row, c_s, c_r)
     start()
-    w2_0, w2_1, w2_2, w2_3, w2_4, w2_5 = weight_reduce(0, col_dev, row_dev, col // 2, False)
-    w2_0(lax.dot_general(small[4], prop_two, TN, preferred_element_type=F32))
+    w2_s, w2_k, w2_1, w2_2, w2_3, w2_4, w2_5, w2_6 = weight_reduce(
+        0, x, y, lambda d: in_col(d, 0), lambda d: in_row(d, 0), False
+    )
+    e_src[0] = lax.dot_general(small[4], prop_two, TN, preferred_element_type=F32).reshape(e_src.shape[1:])
+    w2_s(e_src[0, 1 - core])
 
     def mm2(os, first=False):
         rs_ = [row_at(*o) for o in os]
@@ -384,13 +393,13 @@
     near(2)
     pair()
     mm2([(2, 0), (0, 1)])
+    w2_3()
     for k, d in ((4, -1), (5, 1), (6, 2)):
         f_cp[k].wait_recv()
         to_sibling(ft, (d, 1), 9 + k)
     far(-1)
     far(1)
     mm2([(-1, 1), (1, 1)])
-    w2_3()
     far(2)
 
     last = row_at(2, 1)
@@ -419,24 +428,35 @@
     one()
     for k in range(8, 16):
         s_cp[k].wait_recv()
-    term = None
-    for dx, dz in ring_order:
-        j, jj = col_at(dx, dz, 0), col_at(dx, dz, 1)
-        p = mm(ft[j], acc2[j].astype(BF16)) + mm(ft[jj], sd[jj])
-        term = p if term is None else term + p
-    w1_0, w1_1, w1_2, w1_3, w1_4, w1_5 = weight_reduce(1, row_dev, col_dev, row, True)
-    w1_0(term)
-    w2_4()
+    half_rows = ft.shape[1] // 2
+
+    def term(which):
+        at = pl.ds(pl.multiple_of(which * half_rows, half_rows), half_rows)
+        total = None
+        for dx, dz in ring_order:
+            j, jj = col_at(dx, dz, 0), col_at(dx, dz, 1)
+            p = mm(ft[j, at], acc2[j].astype(BF16)) + mm(ft[jj, at], sd[jj])
+            total = p if total is None else total + p
+        return total
+
+    w1_s, w1_k, w1_1, w1_2, w1_3, w1_4, w1_5, w1_6 = weight_reduce(
+        1, y, x, lambda d: in_row(d, 0), lambda d: in_col(d, 0), True
+    )
+    w1_s(term(1 - core))
+    w1_k(term(core))
     w1_1()
     two()
     w1_2()
     three()
     w1_3()
+    w2_4()
     prop_one = four().astype(BF16)
+    w1_4()
+    w2_5()
     node_out[...] = lax.dot_general(prop_one, small[6], NT, preferred_element_type=F32).astype(BF16)
-    w2_5(wg2_out)
-    w1_4()
-    w1_5(wg1_out)
+    w2_6(wg2_out)
+    w1_5()
+    w1_6(wg1_out)
     for cp in pending:
         cp.wait_send()
 
@@ -461,7 +481,7 @@
     tile = rows // tile_mask.shape[0]
     scale = 4.0 * s ** (-0.5)
     h = s // 2
-    sl = f // n_col
+    sl = f // 8
     dma = pltpu.SemaphoreType.DMA
     outs = pl.pallas_call(
         functools.partial(kernel, n_row, n_col, tile, scale),
@@ -487,18 +507,16 @@
             pltpu.VMEM((n_col, s, f), BF16),
             pltpu.VMEM((n_row, s, f), BF16),
             pltpu.VMEM((14, h, f), BF16),
-            pltpu.VMEM((2, 2, n_row, sl, f), F32),
-            pltpu.VMEM((2, n_row, sl, f), F32),
-            pltpu.VMEM((2, n_row, sl, f), F32),
-            pltpu.VMEM((2, n_row, sl, f), F32),
-            pltpu.VMEM((2, n_row, sl, f), F32),
-            pltpu.VMEM((2, sl, f), F32),
-            pltpu.VMEM((2, 2, n_row, sl, f), F32),
+            pltpu.VMEM((2, 2, 4, sl, f), F32),
+            pltpu.VMEM((2, 4, sl, f), F32),
+            pltpu.VMEM((2, 4, sl, f), BF16),
+            pltpu.VMEM((2, 3, sl, f), BF16),
+            pltpu.VMEM((2, 2, 4, sl, f), BF16),
+            pltpu.VMEM((2, 2, 4, sl, f), BF16),
             dma((8,)), dma((n_col,)), dma((16,)), dma((16,)), dma((7,)), dma((7,)),
             dma((14,)), dma((14,)), dma((14,)), dma((14,)), dma((14,)), dma((14,)),
             dma((8,)), dma((8,)), dma((14,)), dma((14,)),
-            dma((4,)), dma((4,)), dma((2, n_row)), dma((2, n_row)), dma((2, n_row)), dma((2, n_row)),
-            dma((2, 2, n_row)), dma((2, 2, n_row)),
+            dma((4,)), dma((4,)), dma((2, 5, 3)), dma((2, 5, 3)),
         ],
         compiler_params=pltpu.CompilerParams(
             collective_id=0, has_side_effects=True, vmem_limit_bytes=56 << 20

time: 80.3 us -> 77.6 us (0.966)
  Pallas kernels: 79.5 us -> 76.8 us
    pallas_call x1, Pallas kernels: 77.7 us -> 74.9 us  [local(): pl.pallas_call(functools.partial(kernel, n_row, n_col, tile, scale), out_...]
where the time goes in v3:
time: 77.6 us; the launch traced here: 77.4 us
  Pallas kernels  76.8 us (99%)
    pallas_call x1, Pallas kernels, local(): pl.pallas_call(functools.partial(kernel, n_row, n_col, tile, scale), out_...  74.9 us
    pallas_call x1, Pallas kernels, local(): pl.pallas_call(finish, out_shape=tuple((jax.ShapeDtypeStruct(o.shape, o.d...  1.86 us

profile of v3, /device:TPU:1, one launch (start us, length us, event | category | flops | bytes accessed | tf_op | source)
XLA Modules:
  0.0 77.4 jit_solution(10193677043930174514)
XLA Ops:
  0.6 74.9 %shard_map.112 = (bf16[256,256]{1,0:T(8,128)(2,1)}, f32[256,256]{1,0:T(8,128)}, f32[256,256]{1,0:T(8,128)}) custom-call(bf16[4096,2048]{1,0:T(8,128)(2,1)} %adj_hbm.1, s32[16,32]{1,0:T(8,128)} %bitcast.1, bf16[256,256]{1,0:T(8,128)(2,1)} %og_hbm.1, bf16[256,256]{1,0:T(8,128)(2,1)} %p2_hbm.1, bf16[256,256]{1,0:T(8,128)(2,1)} %hid_hbm.1, ...), custom_call_target="tpu_custom_call" | custom-call | tf_op jit(solution)/shard_map/pallas_call | solution.py:486
  75.6 1.9 %shard_map.113 = (bf16[256,256]{1,0:T(8,128)(2,1)}, f32[256,256]{1,0:T(8,128)}, f32[256,256]{1,0:T(8,128)}) custom-call(bf16[256,256]{1,0:T(8,128)(2,1)} %get-tuple-element.6.node_in, f32[256,256]{1,0:T(8,128)} %get-tuple-element.7.wg1_in, f32[256,256]{1,0:T(8,128)} %get-tuple-element.8.wg2_in), custom_call_target="tpu_custom_call" | custom-call | tf_op jit(solution)/shard_map/pallas_call | solution.py:525
